TPU v7x, 32 devices: a whole 2x2x4 slice. The times are simulated.
32 devices in a mesh: series: 4 (over y, x), tm: 8 (over z, core).
Axes of the slice: x: 2, y: 2, z: 4, core: 2. Of those that a mesh axis runs over, the one named last changes fastest.
Arguments:
- observed: bfloat16 [8192, 8192], P('series', 'tm'), may hold values from -6 to 6
- mask: bfloat16 [8192, 8192], P('series', 'tm'), may hold values from 0 to 1, as said below
- loadings: float32 [8192, 128], P('series'), may hold values from -0.5 to 0.5
- factors: float32 [8192, 128], P('tm'), may hold values from -6 to 6
- lag_weights: float32 [2, 128], replicated, may hold values from 0.2 to 0.7
Outputs:
- new_loadings: float32 [8192, 128], P('series')
- new_factors: float32 [8192, 128], P('tm')
Inputs may be any that keep to these rules, and one draw needn't show every extreme that they name: `mask`: each entry is 0 or 1.
All inputs are finite; a program needn't handle non-finite values.
Results may differ from a plain program's by a relative error of at most 0.0041.
Values sent between devices are 32-bit elements; how exact they have to be, the bound alone decides.
No kernel may reach another device: no remote copies, remote signals or barrier semaphores. Data moves between devices by JAX's collectives and lax.ppermute only.
A program may use at most 128 MiB of HBM per device.

v0:
```python
import jax
import jax.numpy as jnp
from jax import lax
from jax.sharding import PartitionSpec as P

LAG = 1440
OUTER = 2
TIME_STEPS = 2
smooth = 4.0
shrink = 0.1
margin = 32.0


def shifted(value, axis, steps):
    count = lax.axis_size(axis)
    initial, last = (max(0, -steps), min(count, count - steps))
    return lax.ppermute(value, axis, [(source, source + steps) for source in range(initial, last)])


def tile_residual(observed, mask, fb, xb):
    prod = lax.dot_general(fb, xb, (((1,), (1,)), ((), ())), preferred_element_type=jnp.float32)
    return (mask.astype(jnp.float32) * (prod - observed.astype(jnp.float32))).astype(jnp.bfloat16)


def smoothing(times, lag_weights):
    minutes = times.shape[0]
    whole = LAG // minutes
    rest = LAG % minutes
    before_one = jnp.concatenate(
        [shifted(times[minutes - 1 :], "tm", 1), times[: minutes - 1]], axis=0
    )
    before_far = jnp.concatenate(
        [
            shifted(times[minutes - rest :], "tm", whole + 1),
            shifted(times[: minutes - rest], "tm", whole),
        ],
        axis=0,
    )
    resid = times - lag_weights[0] * before_one - lag_weights[1] * before_far
    after_one = jnp.concatenate([resid[1:], shifted(resid[:1], "tm", -1)], axis=0)
    after_far = jnp.concatenate(
        [shifted(resid[rest:], "tm", -whole), shifted(resid[:rest], "tm", -(whole + 1))], axis=0
    )
    return smooth * (resid - lag_weights[0] * after_one - lag_weights[1] * after_far)


def body(observed, mask, loadings, factors, lag_weights):
    total_series = loadings.shape[0] * lax.axis_size("series")
    total_minutes = factors.shape[0] * lax.axis_size("tm")
    rank_width = loadings.shape[1]
    step_time = 1.0 / (total_series / rank_width + margin)
    step_load = 1.0 / total_minutes
    loads = loadings
    times = factors
    for outer in range(OUTER):
        fb = loads.astype(jnp.bfloat16)
        for inner in range(TIME_STEPS):
            xb = times.astype(jnp.bfloat16)
            rb = tile_residual(observed, mask, fb, xb)
            partial_grad = lax.dot_general(
                rb, fb, (((0,), (0,)), ((), ())), preferred_element_type=jnp.float32
            )
            smooth_grad = smoothing(times, lag_weights)
            share = lax.psum_scatter(partial_grad, "series", scatter_dimension=0, tiled=True)
            rows = share.shape[0]
            start = lax.axis_index("series") * rows
            own = lax.dynamic_slice_in_dim(times, start, rows, 0)
            own_smooth = lax.dynamic_slice_in_dim(smooth_grad, start, rows, 0)
            updated = own - step_time * (share + own_smooth)
            times = lax.all_gather(updated, "series", axis=0, tiled=True)
        xb = times.astype(jnp.bfloat16)
        rb = tile_residual(observed, mask, fb, xb)
        partial_load = jnp.dot(rb, xb, preferred_element_type=jnp.float32)
        grad_f = lax.psum(partial_load, "tm")
        loads = loads - step_load * (grad_f + shrink * loads)
    return (loads, times)


def solution(mesh):
    in_specs = (P("series", "tm"), P("series", "tm"), P("series", None), P("tm", None), P())
    out_specs = (P("series", None), P("tm", None))
    return jax.shard_map(body, mesh=mesh, in_specs=in_specs, out_specs=out_specs, check_vma=False)
```

profile of v0, /device:TPU:0, one launch (start us, length us, event | category | flops | bytes accessed | tf_op | source)
XLA Modules:
  0.0 333.9 jit_solution(2569922140256793986)
XLA Ops:
  7.2 9.1 %fusion.11 = f32[1024,128]{1,0:T(8,128)} fusion(bf16[2048,1024]{1,0:T(8,128)(2,1)} %param.6, bf16[2048,1024]{1,0:T(8,128)(2,1)} %param.5, f32[1024,128]{1,0:T(8,128)} %param.8, f32[2048,128]{1,0:T(8,128)} %param.7), kind=kOutput, calls=%fused_computation.23 | convolution fusion | flops 1084882944 | bytes 10485760 | tf_op jit(solution)/shard_map/dot_general | solution.py:60
  16.4 2.5 collective-permute-start.2
  19.0 4.6 %collective-permute-start = (f32[1,128]{1,0:T(1,128)S(1)}, f32[1,128]{1,0:T(1,128)S(1)}, u32[]{:S(2)}, u32[]{:S(2)}) collective-permute-start(f32[1,128]{1,0:T(1,128)S(1)} %slice.117), channel_id=1, source_target_pairs={{0,1},{1,2},{2,3},{3,4},{4,5},{5,6},{6,7},{8,9},{9,10},{10,11},{11... | collective-permute-start | bytes 1544 | tf_op jit(solution)/shard_map/ppermute | solution.py:17
  23.6 3.5 %collective-permute-start.1 = (f32[416,128]{1,0:T(8,128)S(1)}, f32[416,128]{1,0:T(8,128)S(1)}, u32[]{:S(2)}, u32[]{:S(2)}) collective-permute-start(f32[416,128]{1,0:T(8,128)S(1)} %slice.120), channel_id=1, source_target_pairs={{0,2},{1,3},{2,4},{3,5},{4,6},{5,7},{8,10},{9,11},{10,12},{11,13},... | collective-permute-start | bytes 638984 | tf_op jit(solution)/shard_map/ppermute | solution.py:17
  27.1 4.6 %collective-permute-done.1 = f32[416,128]{1,0:T(8,128)S(1)} collective-permute-done((f32[416,128]{1,0:T(8,128)S(1)}, f32[416,128]{1,0:T(8,128)S(1)}, u32[]{:S(2)}, u32[]{:S(2)}) %collective-permute-start.1) | collective-permute-done | bytes 213024 | tf_op jit(solution)/shard_map/ppermute | solution.py:17
  31.7 0.1 fusion.13
  31.9 1.3 collective-permute-start.4
  33.2 0.7 slice.153
  33.9 1.3 collective-permute-start.5
  35.2 1.3 collective-permute-start.3
  36.5 2.3 collective-permute-done.3
  38.9 6.8 %collective-permute-done.5 = f32[416,128]{1,0:T(8,128)S(1)} collective-permute-done((f32[416,128]{1,0:T(8,128)}, f32[416,128]{1,0:T(8,128)S(1)}, u32[]{:S(2)}, u32[]{:S(2)}) %collective-permute-start.5) | collective-permute-done | bytes 213024 | tf_op jit(solution)/shard_map/ppermute | solution.py:17
  45.7 1.1 fusion.65
  46.8 10.0 %all_gather.12 = f32[1024,128]{1,0:T(8,128)S(1)} all-gather(f32[256,128]{1,0:T(8,128)S(1)} %fusion.65), channel_id=1, replica_groups=mesh['series'=4,'tm'=8] {'series'}, dimensions={0}, use_global_device_ids=true | all-gather | bytes 655360 | tf_op jit(solution)/shard_map/all_gather | solution.py:70
  56.8 8.2 %fusion.10 = f32[1024,128]{1,0:T(8,128)} fusion(bf16[2048,1024]{1,0:T(8,128)(2,1)} %param.6, bf16[2048,1024]{1,0:T(8,128)(2,1)} %param.5, f32[1024,128]{1,0:T(8,128)S(1)} %all_gather.12, f32[2048,128]{1,0:T(8,128)S(1)} %copy-done), kind=kOutput, calls=%fused_computation.22 | convolution fusion | flops 1084882944 | bytes 10485760 | tf_op jit(solution)/shard_map/dot_general | solution.py:60
  65.2 1.3 collective-permute-start.8
  66.5 4.1 %collective-permute-start.7 = (f32[416,128]{1,0:T(8,128)S(1)}, f32[416,128]{1,0:T(8,128)S(1)}, u32[]{:S(2)}, u32[]{:S(2)}) collective-permute-start(f32[416,128]{1,0:T(8,128)S(1)} %slice.156), channel_id=1, source_target_pairs={{0,2},{1,3},{2,4},{3,5},{4,6},{5,7},{8,10},{9,11},{10,12},{11,13},... | collective-permute-start | bytes 638984 | tf_op jit(solution)/shard_map/ppermute | solution.py:17
  70.6 2.8 collective-permute-start.6
  73.4 0.8 collective-permute-done.6
  74.2 2.0 collective-permute-done.7
  76.2 0.1 fusion.15
  76.4 1.3 collective-permute-start.10
  77.7 1.3 collective-permute-start.11
  79.0 1.3 collective-permute-start.9
  80.4 2.8 collective-permute-done.9
  83.2 7.9 %collective-permute-done.11 = f32[416,128]{1,0:T(8,128)S(1)} collective-permute-done((f32[416,128]{1,0:T(8,128)S(1)}, f32[416,128]{1,0:T(8,128)S(1)}, u32[]{:S(2)}, u32[]{:S(2)}) %collective-permute-start.11) | collective-permute-done | bytes 213024 | tf_op jit(solution)/shard_map/ppermute | solution.py:17
  91.0 1.1 fusion.55
  92.1 10.0 %all_gather.13 = f32[1024,128]{1,0:T(8,128)S(1)} all-gather(f32[256,128]{1,0:T(8,128)S(1)} %fusion.55), channel_id=1, replica_groups=mesh['series'=4,'tm'=8] {'series'}, dimensions={0}, use_global_device_ids=true | all-gather | bytes 655360 | tf_op jit(solution)/shard_map/all_gather | solution.py:70
  102.1 6.9 %fusion.7 = f32[2048,128]{1,0:T(8,128)} fusion(bf16[2048,1024]{1,0:T(8,128)(2,1)} %param.6, bf16[2048,1024]{1,0:T(8,128)(2,1)} %param.5, f32[1024,128]{1,0:T(8,128)S(1)} %all_gather.13, f32[2048,128]{1,0:T(8,128)S(1)} %copy-done), kind=kOutput, calls=%fused_computation.19 | convolution fusion | flops 1084751872 | bytes 11010048 | tf_op jit(solution)/shard_map/dot_general | solution.py:73
  109.0 0.2 reduce-scatter.9.cloned.1.call-start
  109.2 57.6 %all-reduce.3.cloned.1.call-done = f32[2048,128]{1,0:T(8,128)} async-done(((f32[2048,128]{1,0:T(8,128)}), f32[2048,128]{1,0:T(8,128)}) %all-reduce.3.cloned.1.call-update) | async-done | bytes 1048592 | tf_op jit(solution)/shard_map/psum | solution.py:74
  166.9 1.4 fusion.20
  168.3 8.2 %fusion.9 = f32[1024,128]{1,0:T(8,128)} fusion(bf16[2048,128]{1,0:T(8,128)(2,1)S(1)} %fusion.20, bf16[2048,1024]{1,0:T(8,128)(2,1)} %param.6, bf16[2048,1024]{1,0:T(8,128)(2,1)} %param.5, f32[1024,128]{1,0:T(8,128)S(1)} %all_gather.13), kind=kOutput, calls=%fused_computation.21 | convolution fusion | flops 1084358656 | bytes 9961472 | tf_op jit(solution)/shard_map/dot_general | solution.py:60
  176.6 1.3 collective-permute-start.14
  178.0 3.2 collective-permute-start.13
  181.2 3.1 collective-permute-start.12
  184.3 0.8 collective-permute-done.12
  185.1 1.7 collective-permute-done.13
  186.8 0.1 fusion.17
  186.9 1.3 collective-permute-start.16
  188.2 1.3 collective-permute-start.17
  189.6 1.3 collective-permute-start.15
  190.9 2.8 collective-permute-done.15
  193.7 8.0 %collective-permute-done.17 = f32[416,128]{1,0:T(8,128)} collective-permute-done((f32[416,128]{1,0:T(8,128)S(1)}, f32[416,128]{1,0:T(8,128)}, u32[]{:S(2)}, u32[]{:S(2)}) %collective-permute-start.17) | collective-permute-done | bytes 213024 | tf_op jit(solution)/shard_map/ppermute | solution.py:17
  201.7 1.0 fusion.45
  202.7 10.0 %all_gather.14 = f32[1024,128]{1,0:T(8,128)S(1)} all-gather(f32[256,128]{1,0:T(8,128)S(1)} %fusion.45), channel_id=1, replica_groups=mesh['series'=4,'tm'=8] {'series'}, dimensions={0}, use_global_device_ids=true | all-gather | bytes 655360 | tf_op jit(solution)/shard_map/all_gather | solution.py:70
  212.8 8.2 %fusion.8 = f32[1024,128]{1,0:T(8,128)} fusion(bf16[2048,128]{1,0:T(8,128)(2,1)S(1)} %fusion.20, bf16[2048,1024]{1,0:T(8,128)(2,1)} %param.6, bf16[2048,1024]{1,0:T(8,128)(2,1)} %param.5, f32[1024,128]{1,0:T(8,128)S(1)} %all_gather.14), kind=kOutput, calls=%fused_computation.20 | convolution fusion | flops 1084358656 | bytes 9961472 | tf_op jit(solution)/shard_map/dot_general | solution.py:60
  221.1 1.3 collective-permute-start.20
  222.5 4.3 %collective-permute-start.19 = (f32[416,128]{1,0:T(8,128)S(1)}, f32[416,128]{1,0:T(8,128)S(1)}, u32[]{:S(2)}, u32[]{:S(2)}) collective-permute-start(f32[416,128]{1,0:T(8,128)S(1)} %slice.172), channel_id=1, source_target_pairs={{0,2},{1,3},{2,4},{3,5},{4,6},{5,7},{8,10},{9,11},{10,12},{11,13},... | collective-permute-start | bytes 638984 | tf_op jit(solution)/shard_map/ppermute | solution.py:17
  226.8 3.1 collective-permute-start.18
  229.9 0.8 collective-permute-done.18
  230.7 1.7 collective-permute-done.19
  232.4 0.1 fusion.19
  232.5 1.3 collective-permute-start.22
  233.9 1.3 collective-permute-start.23
  235.2 1.3 collective-permute-start.21
  236.5 2.8 collective-permute-done.21
  239.3 8.0 %collective-permute-done.23 = f32[416,128]{1,0:T(8,128)} collective-permute-done((f32[416,128]{1,0:T(8,128)S(1)}, f32[416,128]{1,0:T(8,128)}, u32[]{:S(2)}, u32[]{:S(2)}) %collective-permute-start.23) | collective-permute-done | bytes 213024 | tf_op jit(solution)/shard_map/ppermute | solution.py:17
  247.3 1.0 fusion.35
  248.3 10.1 %all_gather.15 = f32[1024,128]{1,0:T(8,128)S(1)} all-gather(f32[256,128]{1,0:T(8,128)S(1)} %fusion.35), channel_id=1, replica_groups=mesh['series'=4,'tm'=8] {'series'}, dimensions={0}, use_global_device_ids=true | all-gather | bytes 655360 | tf_op jit(solution)/shard_map/all_gather | solution.py:70
  258.4 7.0 %fusion.6 = f32[2048,128]{1,0:T(8,128)} fusion(bf16[2048,1024]{1,0:T(8,128)(2,1)} %param.6, bf16[2048,1024]{1,0:T(8,128)(2,1)} %param.5, bf16[2048,128]{1,0:T(8,128)(2,1)S(1)} %fusion.20, f32[1024,128]{1,0:T(8,128)S(1)} %all_gather.15), kind=kOutput, calls=%fused_computation.18 | convolution fusion | flops 1084489728 | bytes 10485760 | tf_op jit(solution)/shard_map/dot_general | solution.py:73
  265.4 58.4 %all-reduce.5.cloned.1.call-done = f32[2048,128]{1,0:T(8,128)} async-done(((f32[2048,128]{1,0:T(8,128)}), f32[2048,128]{1,0:T(8,128)}) %all-reduce.5.cloned.1.call-update) | async-done | bytes 1048592 | tf_op jit(solution)/shard_map/psum | solution.py:74
  323.8 2.5 multiply_subtract_fusion
  326.3 0.8 copy.10
  (60 shorter events, 0.8 us)
Async XLA Ops:
  7.2 9.2 %copy-start.1 = (f32[1024,128]{1,0:T(8,128)S(1)}, f32[1024,128]{1,0:T(8,128)}, u32[]{:S(2)}) copy-start(f32[1024,128]{1,0:T(8,128)} %param.8) | copy-start | bytes 1572868
  7.2 19.9 %copy-start.3 = (f32[2,128]{1,0:T(2,128)S(1)}, f32[2,128]{1,0:T(2,128)}, u32[]{:S(2)}) copy-start(f32[2,128]{1,0:T(2,128)} %param.9) | copy-start | bytes 3076
  7.2 38.5 %reduce-scatter.5.cloned.1.call-start = ((), (), s32[]{:S(2)}) async-start(), calls=%async_computation.4 | async-start | bytes 655360 | tf_op jit(solution)/shard_map/reduce_scatter | solution.py:64
  16.3 40.5 %copy-start = (f32[2048,128]{1,0:T(8,128)S(1)}, f32[2048,128]{1,0:T(8,128)}, u32[]{:S(2)}) copy-start(f32[2048,128]{1,0:T(8,128)} %param.7) | copy-start | bytes 3145732
  16.3 74.7 %reduce-scatter.7.cloned.1.call-start = ((), (), s32[]{:S(2)}) async-start(), calls=%async_computation.5 | async-start | bytes 655360 | tf_op jit(solution)/shard_map/reduce_scatter | solution.py:64
  16.4 15.3 %collective-permute-start.2 = (f32[608,128]{1,0:T(8,128)S(1)}, f32[608,128]{1,0:T(8,128)S(1)}, u32[]{:S(2)}, u32[]{:S(2)}) collective-permute-start(f32[608,128]{1,0:T(8,128)S(1)} %slice.121), channel_id=1, source_target_pairs={{0,1},{1,2},{2,3},{3,4},{4,5},{5,6},{6,7},{8,9},{9,10},{10,11},{11... | collective-permute-start | bytes 933896 | tf_op jit(solution)/shard_map/ppermute | solution.py:17
  19.0 8.1 %collective-permute-start = (f32[1,128]{1,0:T(1,128)S(1)}, f32[1,128]{1,0:T(1,128)S(1)}, u32[]{:S(2)}, u32[]{:S(2)}) collective-permute-start(f32[1,128]{1,0:T(1,128)S(1)} %slice.117), channel_id=1, source_target_pairs={{0,1},{1,2},{2,3},{3,4},{4,5},{5,6},{6,7},{8,9},{9,10},{10,11},{11... | collective-permute-start | bytes 1544 | tf_op jit(solution)/shard_map/ppermute | solution.py:17
  23.6 8.2 %collective-permute-start.1 = (f32[416,128]{1,0:T(8,128)S(1)}, f32[416,128]{1,0:T(8,128)S(1)}, u32[]{:S(2)}, u32[]{:S(2)}) collective-permute-start(f32[416,128]{1,0:T(8,128)S(1)} %slice.120), channel_id=1, source_target_pairs={{0,2},{1,3},{2,4},{3,5},{4,6},{5,7},{8,10},{9,11},{10,12},{11,13},... | collective-permute-start | bytes 638984 | tf_op jit(solution)/shard_map/ppermute | solution.py:17
  31.9 13.8 %collective-permute-start.4 = (f32[608,128]{1,0:T(8,128)S(1)}, f32[608,128]{1,0:T(8,128)S(1)}, u32[]{:S(2)}, u32[]{:S(2)}) collective-permute-start(f32[608,128]{1,0:T(8,128)S(1)} %slice.152), channel_id=1, source_target_pairs={{1,0},{2,1},{3,2},{4,3},{5,4},{6,5},{7,6},{9,8},{10,9},{11,10},{12... | collective-permute-start | bytes 933896 | tf_op jit(solution)/shard_map/ppermute | solution.py:17
  33.9 11.8 %collective-permute-start.5 = (f32[416,128]{1,0:T(8,128)}, f32[416,128]{1,0:T(8,128)S(1)}, u32[]{:S(2)}, u32[]{:S(2)}) collective-permute-start(f32[416,128]{1,0:T(8,128)} %slice.153), channel_id=1, source_target_pairs={{2,0},{3,1},{4,2},{5,3},{6,4},{7,5},{10,8},{11,9},{12,10},{13,11},... | collective-permute-start | bytes 638984 | tf_op jit(solution)/shard_map/ppermute | solution.py:17
  35.2 3.7 %collective-permute-start.3 = (f32[1,128]{1,0:T(1,128)S(1)}, f32[1,128]{1,0:T(1,128)S(1)}, u32[]{:S(2)}, u32[]{:S(2)}) collective-permute-start(f32[1,128]{1,0:T(1,128)S(1)} %slice.151), channel_id=1, source_target_pairs={{1,0},{2,1},{3,2},{4,3},{5,4},{6,5},{7,6},{9,8},{10,9},{11,10},{12... | collective-permute-start | bytes 1544 | tf_op jit(solution)/shard_map/ppermute | solution.py:17
  65.1 101.8 %all-reduce.3.cloned.1.call-start = ((), (), s32[]{:S(2)}) async-start(), calls=%async_computation.6 | async-start | bytes 2097152 | tf_op jit(solution)/shard_map/psum | solution.py:74
  65.2 11.1 %collective-permute-start.8 = (f32[608,128]{1,0:T(8,128)S(1)}, f32[608,128]{1,0:T(8,128)S(1)}, u32[]{:S(2)}, u32[]{:S(2)}) collective-permute-start(f32[608,128]{1,0:T(8,128)S(1)} %slice.157), channel_id=1, source_target_pairs={{0,1},{1,2},{2,3},{3,4},{4,5},{5,6},{6,7},{8,9},{9,10},{10,11},{11... | collective-permute-start | bytes 933896 | tf_op jit(solution)/shard_map/ppermute | solution.py:17
  66.5 9.7 %collective-permute-start.7 = (f32[416,128]{1,0:T(8,128)S(1)}, f32[416,128]{1,0:T(8,128)S(1)}, u32[]{:S(2)}, u32[]{:S(2)}) collective-permute-start(f32[416,128]{1,0:T(8,128)S(1)} %slice.156), channel_id=1, source_target_pairs={{0,2},{1,3},{2,4},{3,5},{4,6},{5,7},{8,10},{9,11},{10,12},{11,13},... | collective-permute-start | bytes 638984 | tf_op jit(solution)/shard_map/ppermute | solution.py:17
  70.6 3.6 %collective-permute-start.6 = (f32[1,128]{1,0:T(1,128)S(1)}, f32[1,128]{1,0:T(1,128)S(1)}, u32[]{:S(2)}, u32[]{:S(2)}) collective-permute-start(f32[1,128]{1,0:T(1,128)S(1)} %slice.154), channel_id=1, source_target_pairs={{0,1},{1,2},{2,3},{3,4},{4,5},{5,6},{6,7},{8,9},{9,10},{10,11},{11... | collective-permute-start | bytes 1544 | tf_op jit(solution)/shard_map/ppermute | solution.py:17
  76.4 14.6 %collective-permute-start.10 = (f32[608,128]{1,0:T(8,128)S(1)}, f32[608,128]{1,0:T(8,128)S(1)}, u32[]{:S(2)}, u32[]{:S(2)}) collective-permute-start(f32[608,128]{1,0:T(8,128)S(1)} %slice.160), channel_id=1, source_target_pairs={{1,0},{2,1},{3,2},{4,3},{5,4},{6,5},{7,6},{9,8},{10,9},{11,10},{12... | collective-permute-start | bytes 933896 | tf_op jit(solution)/shard_map/ppermute | solution.py:17
  77.7 13.3 %collective-permute-start.11 = (f32[416,128]{1,0:T(8,128)S(1)}, f32[416,128]{1,0:T(8,128)S(1)}, u32[]{:S(2)}, u32[]{:S(2)}) collective-permute-start(f32[416,128]{1,0:T(8,128)S(1)} %slice.161), channel_id=1, source_target_pairs={{2,0},{3,1},{4,2},{5,3},{6,4},{7,5},{10,8},{11,9},{12,10},{13,11},... | collective-permute-start | bytes 638984 | tf_op jit(solution)/shard_map/ppermute | solution.py:17
  79.0 4.2 %collective-permute-start.9 = (f32[1,128]{1,0:T(1,128)S(1)}, f32[1,128]{1,0:T(1,128)S(1)}, u32[]{:S(2)}, u32[]{:S(2)}) collective-permute-start(f32[1,128]{1,0:T(1,128)S(1)} %slice.159), channel_id=1, source_target_pairs={{1,0},{2,1},{3,2},{4,3},{5,4},{6,5},{7,6},{9,8},{10,9},{11,10},{12... | collective-permute-start | bytes 1544 | tf_op jit(solution)/shard_map/ppermute | solution.py:17
  109.0 92.7 %reduce-scatter.9.cloned.1.call-start = ((), (), s32[]{:S(2)}) async-start(), calls=%async_computation.7 | async-start | bytes 655360 | tf_op jit(solution)/shard_map/reduce_scatter | solution.py:64
  176.6 70.7 %reduce-scatter.11.cloned.1.call-start = ((), (), s32[]{:S(2)}) async-start(), calls=%async_computation.8 | async-start | bytes 655360 | tf_op jit(solution)/shard_map/reduce_scatter | solution.py:64
  176.6 10.1 %collective-permute-start.14 = (f32[608,128]{1,0:T(8,128)S(1)}, f32[608,128]{1,0:T(8,128)S(1)}, u32[]{:S(2)}, u32[]{:S(2)}) collective-permute-start(f32[608,128]{1,0:T(8,128)S(1)} %slice.165), channel_id=1, source_target_pairs={{0,1},{1,2},{2,3},{3,4},{4,5},{5,6},{6,7},{8,9},{9,10},{10,11},{11... | collective-permute-start | bytes 933896 | tf_op jit(solution)/shard_map/ppermute | solution.py:17
  178.0 8.8 %collective-permute-start.13 = (f32[416,128]{1,0:T(8,128)S(1)}, f32[416,128]{1,0:T(8,128)S(1)}, u32[]{:S(2)}, u32[]{:S(2)}) collective-permute-start(f32[416,128]{1,0:T(8,128)S(1)} %slice.164), channel_id=1, source_target_pairs={{0,2},{1,3},{2,4},{3,5},{4,6},{5,7},{8,10},{9,11},{10,12},{11,13},... | collective-permute-start | bytes 638984 | tf_op jit(solution)/shard_map/ppermute | solution.py:17
  181.2 3.9 %collective-permute-start.12 = (f32[1,128]{1,0:T(1,128)S(1)}, f32[1,128]{1,0:T(1,128)S(1)}, u32[]{:S(2)}, u32[]{:S(2)}) collective-permute-start(f32[1,128]{1,0:T(1,128)S(1)} %slice.162), channel_id=1, source_target_pairs={{0,1},{1,2},{2,3},{3,4},{4,5},{5,6},{6,7},{8,9},{9,10},{10,11},{11... | collective-permute-start | bytes 1544 | tf_op jit(solution)/shard_map/ppermute | solution.py:17
  186.9 14.8 %collective-permute-start.16 = (f32[608,128]{1,0:T(8,128)S(1)}, f32[608,128]{1,0:T(8,128)S(1)}, u32[]{:S(2)}, u32[]{:S(2)}) collective-permute-start(f32[608,128]{1,0:T(8,128)S(1)} %slice.168), channel_id=1, source_target_pairs={{1,0},{2,1},{3,2},{4,3},{5,4},{6,5},{7,6},{9,8},{10,9},{11,10},{12... | collective-permute-start | bytes 933896 | tf_op jit(solution)/shard_map/ppermute | solution.py:17
  188.2 13.4 %collective-permute-start.17 = (f32[416,128]{1,0:T(8,128)S(1)}, f32[416,128]{1,0:T(8,128)}, u32[]{:S(2)}, u32[]{:S(2)}) collective-permute-start(f32[416,128]{1,0:T(8,128)S(1)} %slice.169), channel_id=1, source_target_pairs={{2,0},{3,1},{4,2},{5,3},{6,4},{7,5},{10,8},{11,9},{12,10},{13,11},... | collective-permute-start | bytes 638984 | tf_op jit(solution)/shard_map/ppermute | solution.py:17
  189.6 4.2 %collective-permute-start.15 = (f32[1,128]{1,0:T(1,128)S(1)}, f32[1,128]{1,0:T(1,128)S(1)}, u32[]{:S(2)}, u32[]{:S(2)}) collective-permute-start(f32[1,128]{1,0:T(1,128)S(1)} %slice.167), channel_id=1, source_target_pairs={{1,0},{2,1},{3,2},{4,3},{5,4},{6,5},{7,6},{9,8},{10,9},{11,10},{12... | collective-permute-start | bytes 1544 | tf_op jit(solution)/shard_map/ppermute | solution.py:17
  221.0 102.7 %all-reduce.5.cloned.1.call-start = ((), (), s32[]{:S(2)}) async-start(), calls=%async_computation.9 | async-start | bytes 2097152 | tf_op jit(solution)/shard_map/psum | solution.py:74
  221.1 11.3 %collective-permute-start.20 = (f32[608,128]{1,0:T(8,128)S(1)}, f32[608,128]{1,0:T(8,128)S(1)}, u32[]{:S(2)}, u32[]{:S(2)}) collective-permute-start(f32[608,128]{1,0:T(8,128)S(1)} %slice.173), channel_id=1, source_target_pairs={{0,1},{1,2},{2,3},{3,4},{4,5},{5,6},{6,7},{8,9},{9,10},{10,11},{11... | collective-permute-start | bytes 933896 | tf_op jit(solution)/shard_map/ppermute | solution.py:17
  222.5 9.9 %collective-permute-start.19 = (f32[416,128]{1,0:T(8,128)S(1)}, f32[416,128]{1,0:T(8,128)S(1)}, u32[]{:S(2)}, u32[]{:S(2)}) collective-permute-start(f32[416,128]{1,0:T(8,128)S(1)} %slice.172), channel_id=1, source_target_pairs={{0,2},{1,3},{2,4},{3,5},{4,6},{5,7},{8,10},{9,11},{10,12},{11,13},... | collective-permute-start | bytes 638984 | tf_op jit(solution)/shard_map/ppermute | solution.py:17
  226.8 3.9 %collective-permute-start.18 = (f32[1,128]{1,0:T(1,128)S(1)}, f32[1,128]{1,0:T(1,128)S(1)}, u32[]{:S(2)}, u32[]{:S(2)}) collective-permute-start(f32[1,128]{1,0:T(1,128)S(1)} %slice.170), channel_id=1, source_target_pairs={{0,1},{1,2},{2,3},{3,4},{4,5},{5,6},{6,7},{8,9},{9,10},{10,11},{11... | collective-permute-start | bytes 1544 | tf_op jit(solution)/shard_map/ppermute | solution.py:17
  232.5 14.8 %collective-permute-start.22 = (f32[608,128]{1,0:T(8,128)S(1)}, f32[608,128]{1,0:T(8,128)S(1)}, u32[]{:S(2)}, u32[]{:S(2)}) collective-permute-start(f32[608,128]{1,0:T(8,128)S(1)} %slice.176), channel_id=1, source_target_pairs={{1,0},{2,1},{3,2},{4,3},{5,4},{6,5},{7,6},{9,8},{10,9},{11,10},{12... | collective-permute-start | bytes 933896 | tf_op jit(solution)/shard_map/ppermute | solution.py:17
  233.9 13.4 %collective-permute-start.23 = (f32[416,128]{1,0:T(8,128)S(1)}, f32[416,128]{1,0:T(8,128)}, u32[]{:S(2)}, u32[]{:S(2)}) collective-permute-start(f32[416,128]{1,0:T(8,128)S(1)} %slice.177), channel_id=1, source_target_pairs={{2,0},{3,1},{4,2},{5,3},{6,4},{7,5},{10,8},{11,9},{12,10},{13,11},... | collective-permute-start | bytes 638984 | tf_op jit(solution)/shard_map/ppermute | solution.py:17
  235.2 4.2 %collective-permute-start.21 = (f32[1,128]{1,0:T(1,128)S(1)}, f32[1,128]{1,0:T(1,128)S(1)}, u32[]{:S(2)}, u32[]{:S(2)}) collective-permute-start(f32[1,128]{1,0:T(1,128)S(1)} %slice.175), channel_id=1, source_target_pairs={{1,0},{2,1},{3,2},{4,3},{5,4},{6,5},{7,6},{9,8},{10,9},{11,10},{12... | collective-permute-start | bytes 1544 | tf_op jit(solution)/shard_map/ppermute | solution.py:17
  258.4 65.4 %copy-start.2 = (f32[2048,128]{1,0:T(8,128)S(1)}, f32[2048,128]{1,0:T(8,128)}, u32[]{:S(2)}) copy-start(f32[2048,128]{1,0:T(8,128)} %all-reduce.3.cloned.1.call-done) | copy-start | bytes 3145732
Sparse Core Ops, SparseCore 0:
  16.4 27.8 reduce-scatter.4
  65.2 23.8 reduce-scatter.6
  109.1 57.7 all-reduce.2
  176.7 24.1 reduce-scatter.8
  221.2 24.5 reduce-scatter.10
  265.5 58.2 all-reduce.4
where the time goes:
time: 335 us; the launch traced here: 334 us
  waiting for transfers between devices  170 us (51%)
  starting transfers between devices  51 us (15%)
  matrix products  47.7 us (14%)
  blocking collectives  40.2 us (12%)
  between operations  14.6 us (4%)
  other arithmetic  8.5 us (3%)
    psum x2, waiting for transfers between devices, body(): grad_f = lax.psum(partial_load, 'tm')  116 us
    ppermute x24, waiting for transfers between devices, shifted(): lax.ppermute(value, axis, [(source, source + steps) for source in range(i...  53.9 us
    ppermute x24, starting transfers between devices, shifted(): lax.ppermute(value, axis, [(source, source + steps) for source in range(i...  50.6 us
    all_gather x4, blocking collectives, body(): times = lax.all_gather(updated, 'series', axis=0, tiled=True)  40.2 us
    dot_general x4, matrix products, body(): lax.dot_general(rb, fb, (((0,), (0,)), ((), ())), preferred_element_type=...  33.8 us
    dot_general x2, matrix products, body(): partial_load = jnp.dot(rb, xb, preferred_element_type=jnp.float32)  13.9 us
  transfers between devices with their start and end apart: 30, of which 17 were waited for; matrix products, arithmetic and copies ran while one was open for 0% of the time, Pallas kernels for 0%

commit v1 on v0

--- a/solution.py
+++ b/solution.py
@@ -71,7 +71,16 @@
         xb = times.astype(jnp.bfloat16)
         rb = tile_residual(observed, mask, fb, xb)
         partial_load = jnp.dot(rb, xb, preferred_element_type=jnp.float32)
-        grad_f = lax.psum(partial_load, "tm")
+
+        def report_the_islands(dev_axis, base_x):
+            axis_n = lax.axis_size(dev_axis)
+            block_now = base_x
+            w1 = lambda vec_out: [(rr, rr ^ vec_out) for rr in range(axis_n)]
+            for hop_no in range(axis_n.bit_length() - 1):
+                block_now = block_now + lax.ppermute(block_now, dev_axis, w1(1 << hop_no))
+            return block_now
+
+        grad_f = report_the_islands("tm", base_x=partial_load)
         loads = loads - step_load * (grad_f + shrink * loads)
     return (loads, times)
 

time: 335 us -> 364 us (1.087)
  waiting for transfers between devices: 170 us -> 197 us
  starting transfers between devices: 51 us -> 57.1 us
    ppermute x0 -> x6, waiting for transfers between devices: none -> 144 us  [report_the_islands(): block_now = block_now + lax.ppermute(block_now, dev_axis, w1(1 << hop_no))]
    psum x2 -> x0, waiting for transfers between devices: 116 us -> none  [body(): grad_f = lax.psum(partial_load, 'tm')]
    ppermute x0 -> x6, starting transfers between devices: none -> 7.95 us  [report_the_islands(): block_now = block_now + lax.ppermute(block_now, dev_axis, w1(1 << hop_no))]
  transfers between devices with their start and end apart: 30 -> 34, of which waited for: 17 -> 22; matrix products, arithmetic and copies ran while one was open for 0% -> 0% of each run, Pallas kernels for 0% -> 0%
where the time goes in v1:
time: 364 us; the launch traced here: 363 us
  waiting for transfers between devices  197 us (54%)
  starting transfers between devices  57.1 us (16%)
  matrix products  45.5 us (12%)
  blocking collectives  39.9 us (11%)
  between operations  14.3 us (4%)
  other arithmetic  6.56 us (2%)
    ppermute x6, waiting for transfers between devices, report_the_islands(): block_now = block_now + lax.ppermute(block_now, dev_axis, w1(1 << hop_no))  144 us
    ppermute x24, waiting for transfers between devices, shifted(): lax.ppermute(value, axis, [(source, source + steps) for source in range(i...  53.3 us
    ppermute x24, starting transfers between devices, shifted(): lax.ppermute(value, axis, [(source, source + steps) for source in range(i...  49 us
    all_gather x4, blocking collectives, body(): times = lax.all_gather(updated, 'series', axis=0, tiled=True)  39.9 us
    dot_general x4, matrix products, body(): lax.dot_general(rb, fb, (((0,), (0,)), ((), ())), preferred_element_type=...  33.7 us
    dot_general x2, matrix products, body(): partial_load = jnp.dot(rb, xb, preferred_element_type=jnp.float32)  11.8 us
    ppermute x6, starting transfers between devices, report_the_islands(): block_now = block_now + lax.ppermute(block_now, dev_axis, w1(1 << hop_no))  7.95 us
  transfers between devices with their start and end apart: 34, of which 22 were waited for; matrix products, arithmetic and copies ran while one was open for 0% of the time, Pallas kernels for 0%

profile of v1, /device:TPU:0, one launch (start us, length us, event | category | flops | bytes accessed | tf_op | source)
XLA Modules:
  0.0 362.6 jit_solution(10533224339401197446)
XLA Ops:
  7.2 9.0 %fusion.11 = f32[1024,128]{1,0:T(8,128)} fusion(bf16[2048,1024]{1,0:T(8,128)(2,1)} %param.6, bf16[2048,1024]{1,0:T(8,128)(2,1)} %param.5, f32[1024,128]{1,0:T(8,128)} %param.8, f32[2048,128]{1,0:T(8,128)} %param.7), kind=kOutput, calls=%fused_computation.23 | convolution fusion | flops 1084882944 | bytes 10485760 | tf_op jit(solution)/shard_map/dot_general | solution.py:60
  16.3 2.5 collective-permute-start.2
  18.9 4.6 %collective-permute-start = (f32[1,128]{1,0:T(1,128)S(1)}, f32[1,128]{1,0:T(1,128)S(1)}, u32[]{:S(2)}, u32[]{:S(2)}) collective-permute-start(f32[1,128]{1,0:T(1,128)S(1)} %slice.117), channel_id=1, source_target_pairs={{0,1},{1,2},{2,3},{3,4},{4,5},{5,6},{6,7},{8,9},{9,10},{10,11},{11... | collective-permute-start | bytes 1544 | tf_op jit(solution)/shard_map/ppermute | solution.py:17
  23.5 3.5 collective-permute-start.1
  27.0 4.6 %collective-permute-done.1 = f32[416,128]{1,0:T(8,128)S(1)} collective-permute-done((f32[416,128]{1,0:T(8,128)S(1)}, f32[416,128]{1,0:T(8,128)S(1)}, u32[]{:S(2)}, u32[]{:S(2)}) %collective-permute-start.1) | collective-permute-done | bytes 213024 | tf_op jit(solution)/shard_map/ppermute | solution.py:17
  31.8 1.3 collective-permute-start.4
  33.8 1.3 collective-permute-start.5
  35.1 1.3 collective-permute-start.3
  36.4 2.3 collective-permute-done.3
  38.8 6.8 %collective-permute-done.5 = f32[416,128]{1,0:T(8,128)S(1)} collective-permute-done((f32[416,128]{1,0:T(8,128)}, f32[416,128]{1,0:T(8,128)S(1)}, u32[]{:S(2)}, u32[]{:S(2)}) %collective-permute-start.5) | collective-permute-done | bytes 213024 | tf_op jit(solution)/shard_map/ppermute | solution.py:17
  45.6 1.1 fusion.64
  46.7 10.0 %all_gather.12 = f32[1024,128]{1,0:T(8,128)S(1)} all-gather(f32[256,128]{1,0:T(8,128)S(1)} %fusion.64), channel_id=1, replica_groups=mesh['series'=4,'tm'=8] {'series'}, dimensions={0}, use_global_device_ids=true | all-gather | bytes 655360 | tf_op jit(solution)/shard_map/all_gather | solution.py:70
  56.7 8.2 %fusion.10 = f32[1024,128]{1,0:T(8,128)} fusion(bf16[2048,1024]{1,0:T(8,128)(2,1)} %param.6, bf16[2048,1024]{1,0:T(8,128)(2,1)} %param.5, f32[1024,128]{1,0:T(8,128)S(1)} %all_gather.12, f32[2048,128]{1,0:T(8,128)S(1)} %copy-done), kind=kOutput, calls=%fused_computation.22 | convolution fusion | flops 1084882944 | bytes 10485760 | tf_op jit(solution)/shard_map/dot_general | solution.py:60
  65.1 1.3 collective-permute-start.8
  66.4 4.1 %collective-permute-start.7 = (f32[416,128]{1,0:T(8,128)S(1)}, f32[416,128]{1,0:T(8,128)S(1)}, u32[]{:S(2)}, u32[]{:S(2)}) collective-permute-start(f32[416,128]{1,0:T(8,128)S(1)} %slice.156), channel_id=1, source_target_pairs={{0,2},{1,3},{2,4},{3,5},{4,6},{5,7},{8,10},{9,11},{10,12},{11,13},... | collective-permute-start | bytes 638984 | tf_op jit(solution)/shard_map/ppermute | solution.py:17
  70.5 2.8 collective-permute-start.6
  73.3 0.8 collective-permute-done.6
  74.1 2.0 collective-permute-done.7
  76.3 1.3 collective-permute-start.10
  77.6 1.3 collective-permute-start.11
  78.9 1.3 collective-permute-start.9
  80.2 2.8 collective-permute-done.9
  83.1 7.9 %collective-permute-done.11 = f32[416,128]{1,0:T(8,128)S(1)} collective-permute-done((f32[416,128]{1,0:T(8,128)S(1)}, f32[416,128]{1,0:T(8,128)S(1)}, u32[]{:S(2)}, u32[]{:S(2)}) %collective-permute-start.11) | collective-permute-done | bytes 213024 | tf_op jit(solution)/shard_map/ppermute | solution.py:17
  90.9 1.1 fusion.54
  92.0 10.2 %all_gather.13 = f32[1024,128]{1,0:T(8,128)S(1)} all-gather(f32[256,128]{1,0:T(8,128)S(1)} %fusion.54), channel_id=1, replica_groups=mesh['series'=4,'tm'=8] {'series'}, dimensions={0}, use_global_device_ids=true | all-gather | bytes 655360 | tf_op jit(solution)/shard_map/all_gather | solution.py:70
  102.2 5.9 %fusion.7 = f32[2048,128]{1,0:T(8,128)S(1)} fusion(bf16[2048,1024]{1,0:T(8,128)(2,1)} %param.6, bf16[2048,1024]{1,0:T(8,128)(2,1)} %param.5, f32[1024,128]{1,0:T(8,128)S(1)} %all_gather.13, f32[2048,128]{1,0:T(8,128)S(1)} %copy-done), kind=kOutput, calls=%fused_computation.19 | convolution fusion | flops 1084751872 | bytes 11010048 | tf_op jit(solution)/shard_map/dot_general | solution.py:73
  108.2 2.6 collective-permute-done.12
  110.9 1.5 collective-permute-start.13
  112.4 23.8 %collective-permute-done.13 = f32[2048,128]{1,0:T(8,128)S(1)} collective-permute-done((f32[2048,128]{1,0:T(8,128)S(1)}, f32[2048,128]{1,0:T(8,128)S(1)}, u32[]{:S(2)}, u32[]{:S(2)}) %collective-permute-start.13) | collective-permute-done | bytes 1048608 | tf_op jit(solution)/shard_map/ppermute | solution.py:80
  136.3 2.0 collective-permute-start.14
  138.3 45.8 %collective-permute-done.14 = f32[2048,128]{1,0:T(8,128)S(1)} collective-permute-done((f32[2048,128]{1,0:T(8,128)S(1)}, f32[2048,128]{1,0:T(8,128)S(1)}, u32[]{:S(2)}, u32[]{:S(2)}) %collective-permute-start.14) | collective-permute-done | bytes 1048608 | tf_op jit(solution)/shard_map/ppermute | solution.py:80
  184.4 8.2 %fusion.9 = f32[1024,128]{1,0:T(8,128)} fusion(bf16[2048,1024]{1,0:T(8,128)(2,1)} %param.6, bf16[2048,1024]{1,0:T(8,128)(2,1)} %param.5, f32[1024,128]{1,0:T(8,128)S(1)} %all_gather.13, f32[2048,128]{1,0:T(8,128)S(1)} %multiply_subtract_fusion.1), kind=kOutput, calls=%fused_computation.21 | convolution fusion | flops 1084882944 | bytes 10485760 | tf_op jit(solution)/shard_map/dot_general | solution.py:60
  192.7 1.3 collective-permute-start.17
  194.0 1.4 collective-permute-start.16
  195.4 3.0 collective-permute-start.15
  198.4 0.8 collective-permute-done.15
  199.2 1.8 collective-permute-done.16
  201.2 1.3 collective-permute-start.19
  202.5 1.3 collective-permute-start.20
  203.8 1.3 collective-permute-start.18
  205.1 3.0 collective-permute-done.18
  208.2 7.9 %collective-permute-done.20 = f32[416,128]{1,0:T(8,128)S(1)} collective-permute-done((f32[416,128]{1,0:T(8,128)S(1)}, f32[416,128]{1,0:T(8,128)S(1)}, u32[]{:S(2)}, u32[]{:S(2)}) %collective-permute-start.20) | collective-permute-done | bytes 213024 | tf_op jit(solution)/shard_map/ppermute | solution.py:17
  216.2 1.0 fusion.44
  217.2 10.0 %all_gather.14 = f32[1024,128]{1,0:T(8,128)S(1)} all-gather(f32[256,128]{1,0:T(8,128)S(1)} %fusion.44), channel_id=1, replica_groups=mesh['series'=4,'tm'=8] {'series'}, dimensions={0}, use_global_device_ids=true | all-gather | bytes 655360 | tf_op jit(solution)/shard_map/all_gather | solution.py:70
  227.2 8.2 %fusion.8 = f32[1024,128]{1,0:T(8,128)} fusion(bf16[2048,1024]{1,0:T(8,128)(2,1)} %param.6, bf16[2048,1024]{1,0:T(8,128)(2,1)} %param.5, f32[1024,128]{1,0:T(8,128)S(1)} %all_gather.14, f32[2048,128]{1,0:T(8,128)S(1)} %multiply_subtract_fusion.1), kind=kOutput, calls=%fused_computation.20 | convolution fusion | flops 1084882944 | bytes 10485760 | tf_op jit(solution)/shard_map/dot_general | solution.py:60
  235.5 1.3 collective-permute-start.23
  236.9 4.0 %collective-permute-start.22 = (f32[416,128]{1,0:T(8,128)S(1)}, f32[416,128]{1,0:T(8,128)S(1)}, u32[]{:S(2)}, u32[]{:S(2)}) collective-permute-start(f32[416,128]{1,0:T(8,128)S(1)} %slice.172), channel_id=1, source_target_pairs={{0,2},{1,3},{2,4},{3,5},{4,6},{5,7},{8,10},{9,11},{10,12},{11,13},... | collective-permute-start | bytes 638984 | tf_op jit(solution)/shard_map/ppermute | solution.py:17
  240.9 3.5 collective-permute-start.21
  244.4 0.8 collective-permute-done.21
  245.2 1.3 collective-permute-done.22
  246.7 1.3 collective-permute-start.25
  248.0 1.3 collective-permute-start.26
  249.3 1.5 collective-permute-start.24
  250.9 2.6 collective-permute-done.24
  253.5 7.9 %collective-permute-done.26 = f32[416,128]{1,0:T(8,128)S(1)} collective-permute-done((f32[416,128]{1,0:T(8,128)S(1)}, f32[416,128]{1,0:T(8,128)S(1)}, u32[]{:S(2)}, u32[]{:S(2)}) %collective-permute-start.26) | collective-permute-done | bytes 213024 | tf_op jit(solution)/shard_map/ppermute | solution.py:17
  261.3 1.1 fusion.34
  262.4 9.7 %all_gather.15 = f32[1024,128]{1,0:T(8,128)S(1)} all-gather(f32[256,128]{1,0:T(8,128)S(1)} %fusion.34), channel_id=1, replica_groups=mesh['series'=4,'tm'=8] {'series'}, dimensions={0}, use_global_device_ids=true | all-gather | bytes 655360 | tf_op jit(solution)/shard_map/all_gather | solution.py:70
  272.1 5.9 %fusion.6 = f32[2048,128]{1,0:T(8,128)S(1)} fusion(bf16[2048,1024]{1,0:T(8,128)(2,1)} %param.6, bf16[2048,1024]{1,0:T(8,128)(2,1)} %param.5, f32[1024,128]{1,0:T(8,128)S(1)} %all_gather.15, f32[2048,128]{1,0:T(8,128)S(1)} %multiply_subtract_fusion.1), kind=kOutput, calls=%fused_computation.18 | convolution fusion | flops 1084751872 | bytes 11010048 | tf_op jit(solution)/shard_map/dot_general | solution.py:73
  278.1 2.6 collective-permute-done.27
  280.8 1.6 collective-permute-start.28
  282.4 23.7 %collective-permute-done.28 = f32[2048,128]{1,0:T(8,128)S(1)} collective-permute-done((f32[2048,128]{1,0:T(8,128)S(1)}, f32[2048,128]{1,0:T(8,128)S(1)}, u32[]{:S(2)}, u32[]{:S(2)}) %collective-permute-start.28) | collective-permute-done | bytes 1048608 | tf_op jit(solution)/shard_map/ppermute | solution.py:80
  306.2 2.8 collective-permute-start.29
  309.0 45.1 %collective-permute-done.29 = f32[2048,128]{1,0:T(8,128)S(1)} collective-permute-done((f32[2048,128]{1,0:T(8,128)S(1)}, f32[2048,128]{1,0:T(8,128)S(1)}, u32[]{:S(2)}, u32[]{:S(2)}) %collective-permute-start.29) | collective-permute-done | bytes 1048608 | tf_op jit(solution)/shard_map/ppermute | solution.py:80
  354.1 1.2 multiply_subtract_fusion
  (68 shorter events, 3.7 us)
Async XLA Ops:
  7.2 9.1 %copy-start.1 = (f32[1024,128]{1,0:T(8,128)S(1)}, f32[1024,128]{1,0:T(8,128)}, u32[]{:S(2)}) copy-start(f32[1024,128]{1,0:T(8,128)} %param.8) | copy-start | bytes 1572868
  7.2 19.8 %copy-start.2 = (f32[2,128]{1,0:T(2,128)S(1)}, f32[2,128]{1,0:T(2,128)}, u32[]{:S(2)}) copy-start(f32[2,128]{1,0:T(2,128)} %param.9) | copy-start | bytes 3076
  7.2 38.4 %reduce-scatter.5.cloned.1.call-start = ((), (), s32[]{:S(2)}) async-start(), calls=%async_computation.4 | async-start | bytes 655360 | tf_op jit(solution)/shard_map/reduce_scatter | solution.py:64
  16.2 40.5 %copy-start = (f32[2048,128]{1,0:T(8,128)S(1)}, f32[2048,128]{1,0:T(8,128)}, u32[]{:S(2)}) copy-start(f32[2048,128]{1,0:T(8,128)} %param.7) | copy-start | bytes 3145732
  16.2 74.7 %reduce-scatter.7.cloned.1.call-start = ((), (), s32[]{:S(2)}) async-start(), calls=%async_computation.5 | async-start | bytes 655360 | tf_op jit(solution)/shard_map/reduce_scatter | solution.py:64
  16.3 15.3 %collective-permute-start.2 = (f32[608,128]{1,0:T(8,128)S(1)}, f32[608,128]{1,0:T(8,128)S(1)}, u32[]{:S(2)}, u32[]{:S(2)}) collective-permute-start(f32[608,128]{1,0:T(8,128)S(1)} %slice.121), channel_id=1, source_target_pairs={{0,1},{1,2},{2,3},{3,4},{4,5},{5,6},{6,7},{8,9},{9,10},{10,11},{11... | collective-permute-start | bytes 933896 | tf_op jit(solution)/shard_map/ppermute | solution.py:17
  18.9 8.1 %collective-permute-start = (f32[1,128]{1,0:T(1,128)S(1)}, f32[1,128]{1,0:T(1,128)S(1)}, u32[]{:S(2)}, u32[]{:S(2)}) collective-permute-start(f32[1,128]{1,0:T(1,128)S(1)} %slice.117), channel_id=1, source_target_pairs={{0,1},{1,2},{2,3},{3,4},{4,5},{5,6},{6,7},{8,9},{9,10},{10,11},{11... | collective-permute-start | bytes 1544 | tf_op jit(solution)/shard_map/ppermute | solution.py:17
  23.5 8.2 %collective-permute-start.1 = (f32[416,128]{1,0:T(8,128)S(1)}, f32[416,128]{1,0:T(8,128)S(1)}, u32[]{:S(2)}, u32[]{:S(2)}) collective-permute-start(f32[416,128]{1,0:T(8,128)S(1)} %slice.120), channel_id=1, source_target_pairs={{0,2},{1,3},{2,4},{3,5},{4,6},{5,7},{8,10},{9,11},{10,12},{11,13},... | collective-permute-start | bytes 638984 | tf_op jit(solution)/shard_map/ppermute | solution.py:17
  31.8 13.8 %collective-permute-start.4 = (f32[608,128]{1,0:T(8,128)S(1)}, f32[608,128]{1,0:T(8,128)S(1)}, u32[]{:S(2)}, u32[]{:S(2)}) collective-permute-start(f32[608,128]{1,0:T(8,128)S(1)} %slice.152), channel_id=1, source_target_pairs={{1,0},{2,1},{3,2},{4,3},{5,4},{6,5},{7,6},{9,8},{10,9},{11,10},{12... | collective-permute-start | bytes 933896 | tf_op jit(solution)/shard_map/ppermute | solution.py:17
  33.8 11.8 %collective-permute-start.5 = (f32[416,128]{1,0:T(8,128)}, f32[416,128]{1,0:T(8,128)S(1)}, u32[]{:S(2)}, u32[]{:S(2)}) collective-permute-start(f32[416,128]{1,0:T(8,128)} %slice.153), channel_id=1, source_target_pairs={{2,0},{3,1},{4,2},{5,3},{6,4},{7,5},{10,8},{11,9},{12,10},{13,11},... | collective-permute-start | bytes 638984 | tf_op jit(solution)/shard_map/ppermute | solution.py:17
  35.1 3.7 %collective-permute-start.3 = (f32[1,128]{1,0:T(1,128)S(1)}, f32[1,128]{1,0:T(1,128)S(1)}, u32[]{:S(2)}, u32[]{:S(2)}) collective-permute-start(f32[1,128]{1,0:T(1,128)S(1)} %slice.151), channel_id=1, source_target_pairs={{1,0},{2,1},{3,2},{4,3},{5,4},{6,5},{7,6},{9,8},{10,9},{11,10},{12... | collective-permute-start | bytes 1544 | tf_op jit(solution)/shard_map/ppermute | solution.py:17
  65.0 151.2 %reduce-scatter.9.cloned.1.call-start = ((), (), s32[]{:S(2)}) async-start(), calls=%async_computation.6 | async-start | bytes 655360 | tf_op jit(solution)/shard_map/reduce_scatter | solution.py:64
  65.1 11.1 %collective-permute-start.8 = (f32[608,128]{1,0:T(8,128)S(1)}, f32[608,128]{1,0:T(8,128)S(1)}, u32[]{:S(2)}, u32[]{:S(2)}) collective-permute-start(f32[608,128]{1,0:T(8,128)S(1)} %slice.157), channel_id=1, source_target_pairs={{0,1},{1,2},{2,3},{3,4},{4,5},{5,6},{6,7},{8,9},{9,10},{10,11},{11... | collective-permute-start | bytes 933896 | tf_op jit(solution)/shard_map/ppermute | solution.py:17
  66.4 9.7 %collective-permute-start.7 = (f32[416,128]{1,0:T(8,128)S(1)}, f32[416,128]{1,0:T(8,128)S(1)}, u32[]{:S(2)}, u32[]{:S(2)}) collective-permute-start(f32[416,128]{1,0:T(8,128)S(1)} %slice.156), channel_id=1, source_target_pairs={{0,2},{1,3},{2,4},{3,5},{4,6},{5,7},{8,10},{9,11},{10,12},{11,13},... | collective-permute-start | bytes 638984 | tf_op jit(solution)/shard_map/ppermute | solution.py:17
  70.5 3.6 collective-permute-start.6
  76.3 14.6 %collective-permute-start.10 = (f32[608,128]{1,0:T(8,128)S(1)}, f32[608,128]{1,0:T(8,128)S(1)}, u32[]{:S(2)}, u32[]{:S(2)}) collective-permute-start(f32[608,128]{1,0:T(8,128)S(1)} %slice.160), channel_id=1, source_target_pairs={{1,0},{2,1},{3,2},{4,3},{5,4},{6,5},{7,6},{9,8},{10,9},{11,10},{12... | collective-permute-start | bytes 933896 | tf_op jit(solution)/shard_map/ppermute | solution.py:17
  77.6 13.3 %collective-permute-start.11 = (f32[416,128]{1,0:T(8,128)S(1)}, f32[416,128]{1,0:T(8,128)S(1)}, u32[]{:S(2)}, u32[]{:S(2)}) collective-permute-start(f32[416,128]{1,0:T(8,128)S(1)} %slice.161), channel_id=1, source_target_pairs={{2,0},{3,1},{4,2},{5,3},{6,4},{7,5},{10,8},{11,9},{12,10},{13,11},... | collective-permute-start | bytes 638984 | tf_op jit(solution)/shard_map/ppermute | solution.py:17
  78.9 4.2 %collective-permute-start.9 = (f32[1,128]{1,0:T(1,128)S(1)}, f32[1,128]{1,0:T(1,128)S(1)}, u32[]{:S(2)}, u32[]{:S(2)}) collective-permute-start(f32[1,128]{1,0:T(1,128)S(1)} %slice.159), channel_id=1, source_target_pairs={{1,0},{2,1},{3,2},{4,3},{5,4},{6,5},{7,6},{9,8},{10,9},{11,10},{12... | collective-permute-start | bytes 1544 | tf_op jit(solution)/shard_map/ppermute | solution.py:17
  108.1 2.7 collective-permute-start.12
  110.9 25.3 %collective-permute-start.13 = (f32[2048,128]{1,0:T(8,128)S(1)}, f32[2048,128]{1,0:T(8,128)S(1)}, u32[]{:S(2)}, u32[]{:S(2)}) collective-permute-start(f32[2048,128]{1,0:T(8,128)S(1)} %add.57), channel_id=1, source_target_pairs={{0,2},{1,3},{2,0},{3,1},{4,6},{5,7},{6,4},{7,5},{8,10},{9,11},{10,... | collective-permute-start | bytes 3145736 | tf_op jit(solution)/shard_map/ppermute | solution.py:80
  136.3 47.8 %collective-permute-start.14 = (f32[2048,128]{1,0:T(8,128)S(1)}, f32[2048,128]{1,0:T(8,128)S(1)}, u32[]{:S(2)}, u32[]{:S(2)}) collective-permute-start(f32[2048,128]{1,0:T(8,128)S(1)} %add.58), channel_id=1, source_target_pairs={{0,4},{1,5},{2,6},{3,7},{4,0},{5,1},{6,2},{7,3},{8,12},{9,13},{10,... | collective-permute-start | bytes 3145736 | tf_op jit(solution)/shard_map/ppermute | solution.py:80
  192.6 68.7 %reduce-scatter.11.cloned.1.call-start = ((), (), s32[]{:S(2)}) async-start(), calls=%async_computation.7 | async-start | bytes 655360 | tf_op jit(solution)/shard_map/reduce_scatter | solution.py:64
  192.7 8.3 %collective-permute-start.17 = (f32[608,128]{1,0:T(8,128)S(1)}, f32[608,128]{1,0:T(8,128)S(1)}, u32[]{:S(2)}, u32[]{:S(2)}) collective-permute-start(f32[608,128]{1,0:T(8,128)S(1)} %slice.165), channel_id=1, source_target_pairs={{0,1},{1,2},{2,3},{3,4},{4,5},{5,6},{6,7},{8,9},{9,10},{10,11},{11... | collective-permute-start | bytes 933896 | tf_op jit(solution)/shard_map/ppermute | solution.py:17
  194.0 7.0 %collective-permute-start.16 = (f32[416,128]{1,0:T(8,128)S(1)}, f32[416,128]{1,0:T(8,128)S(1)}, u32[]{:S(2)}, u32[]{:S(2)}) collective-permute-start(f32[416,128]{1,0:T(8,128)S(1)} %slice.164), channel_id=1, source_target_pairs={{0,2},{1,3},{2,4},{3,5},{4,6},{5,7},{8,10},{9,11},{10,12},{11,13},... | collective-permute-start | bytes 638984 | tf_op jit(solution)/shard_map/ppermute | solution.py:17
  195.4 3.8 %collective-permute-start.15 = (f32[1,128]{1,0:T(1,128)S(1)}, f32[1,128]{1,0:T(1,128)S(1)}, u32[]{:S(2)}, u32[]{:S(2)}) collective-permute-start(f32[1,128]{1,0:T(1,128)S(1)} %slice.162), channel_id=1, source_target_pairs={{0,1},{1,2},{2,3},{3,4},{4,5},{5,6},{6,7},{8,9},{9,10},{10,11},{11... | collective-permute-start | bytes 1544 | tf_op jit(solution)/shard_map/ppermute | solution.py:17
  201.2 14.9 %collective-permute-start.19 = (f32[608,128]{1,0:T(8,128)S(1)}, f32[608,128]{1,0:T(8,128)S(1)}, u32[]{:S(2)}, u32[]{:S(2)}) collective-permute-start(f32[608,128]{1,0:T(8,128)S(1)} %slice.168), channel_id=1, source_target_pairs={{1,0},{2,1},{3,2},{4,3},{5,4},{6,5},{7,6},{9,8},{10,9},{11,10},{12... | collective-permute-start | bytes 933896 | tf_op jit(solution)/shard_map/ppermute | solution.py:17
  202.5 13.5 %collective-permute-start.20 = (f32[416,128]{1,0:T(8,128)S(1)}, f32[416,128]{1,0:T(8,128)S(1)}, u32[]{:S(2)}, u32[]{:S(2)}) collective-permute-start(f32[416,128]{1,0:T(8,128)S(1)} %slice.169), channel_id=1, source_target_pairs={{2,0},{3,1},{4,2},{5,3},{6,4},{7,5},{10,8},{11,9},{12,10},{13,11},... | collective-permute-start | bytes 638984 | tf_op jit(solution)/shard_map/ppermute | solution.py:17
  203.8 4.4 %collective-permute-start.18 = (f32[1,128]{1,0:T(1,128)S(1)}, f32[1,128]{1,0:T(1,128)S(1)}, u32[]{:S(2)}, u32[]{:S(2)}) collective-permute-start(f32[1,128]{1,0:T(1,128)S(1)} %slice.167), channel_id=1, source_target_pairs={{1,0},{2,1},{3,2},{4,3},{5,4},{6,5},{7,6},{9,8},{10,9},{11,10},{12... | collective-permute-start | bytes 1544 | tf_op jit(solution)/shard_map/ppermute | solution.py:17
  235.5 11.0 %collective-permute-start.23 = (f32[608,128]{1,0:T(8,128)S(1)}, f32[608,128]{1,0:T(8,128)S(1)}, u32[]{:S(2)}, u32[]{:S(2)}) collective-permute-start(f32[608,128]{1,0:T(8,128)S(1)} %slice.173), channel_id=1, source_target_pairs={{0,1},{1,2},{2,3},{3,4},{4,5},{5,6},{6,7},{8,9},{9,10},{10,11},{11... | collective-permute-start | bytes 933896 | tf_op jit(solution)/shard_map/ppermute | solution.py:17
  236.9 9.6 %collective-permute-start.22 = (f32[416,128]{1,0:T(8,128)S(1)}, f32[416,128]{1,0:T(8,128)S(1)}, u32[]{:S(2)}, u32[]{:S(2)}) collective-permute-start(f32[416,128]{1,0:T(8,128)S(1)} %slice.172), channel_id=1, source_target_pairs={{0,2},{1,3},{2,4},{3,5},{4,6},{5,7},{8,10},{9,11},{10,12},{11,13},... | collective-permute-start | bytes 638984 | tf_op jit(solution)/shard_map/ppermute | solution.py:17
  240.9 4.3 %collective-permute-start.21 = (f32[1,128]{1,0:T(1,128)S(1)}, f32[1,128]{1,0:T(1,128)S(1)}, u32[]{:S(2)}, u32[]{:S(2)}) collective-permute-start(f32[1,128]{1,0:T(1,128)S(1)} %slice.170), channel_id=1, source_target_pairs={{0,1},{1,2},{2,3},{3,4},{4,5},{5,6},{6,7},{8,9},{9,10},{10,11},{11... | collective-permute-start | bytes 1544 | tf_op jit(solution)/shard_map/ppermute | solution.py:17
  246.7 14.6 %collective-permute-start.25 = (f32[608,128]{1,0:T(8,128)S(1)}, f32[608,128]{1,0:T(8,128)S(1)}, u32[]{:S(2)}, u32[]{:S(2)}) collective-permute-start(f32[608,128]{1,0:T(8,128)S(1)} %slice.176), channel_id=1, source_target_pairs={{1,0},{2,1},{3,2},{4,3},{5,4},{6,5},{7,6},{9,8},{10,9},{11,10},{12... | collective-permute-start | bytes 933896 | tf_op jit(solution)/shard_map/ppermute | solution.py:17
  248.0 13.3 %collective-permute-start.26 = (f32[416,128]{1,0:T(8,128)S(1)}, f32[416,128]{1,0:T(8,128)S(1)}, u32[]{:S(2)}, u32[]{:S(2)}) collective-permute-start(f32[416,128]{1,0:T(8,128)S(1)} %slice.177), channel_id=1, source_target_pairs={{2,0},{3,1},{4,2},{5,3},{6,4},{7,5},{10,8},{11,9},{12,10},{13,11},... | collective-permute-start | bytes 638984 | tf_op jit(solution)/shard_map/ppermute | solution.py:17
  249.3 4.2 %collective-permute-start.24 = (f32[1,128]{1,0:T(1,128)S(1)}, f32[1,128]{1,0:T(1,128)S(1)}, u32[]{:S(2)}, u32[]{:S(2)}) collective-permute-start(f32[1,128]{1,0:T(1,128)S(1)} %slice.175), channel_id=1, source_target_pairs={{1,0},{2,1},{3,2},{4,3},{5,4},{6,5},{7,6},{9,8},{10,9},{11,10},{12... | collective-permute-start | bytes 1544 | tf_op jit(solution)/shard_map/ppermute | solution.py:17
  278.0 2.7 collective-permute-start.27
  280.8 25.3 %collective-permute-start.28 = (f32[2048,128]{1,0:T(8,128)S(1)}, f32[2048,128]{1,0:T(8,128)S(1)}, u32[]{:S(2)}, u32[]{:S(2)}) collective-permute-start(f32[2048,128]{1,0:T(8,128)S(1)} %add.63), channel_id=1, source_target_pairs={{0,2},{1,3},{2,0},{3,1},{4,6},{5,7},{6,4},{7,5},{8,10},{9,11},{10,... | collective-permute-start | bytes 3145736 | tf_op jit(solution)/shard_map/ppermute | solution.py:80
  306.2 47.9 %collective-permute-start.29 = (f32[2048,128]{1,0:T(8,128)S(1)}, f32[2048,128]{1,0:T(8,128)S(1)}, u32[]{:S(2)}, u32[]{:S(2)}) collective-permute-start(f32[2048,128]{1,0:T(8,128)S(1)} %add.64), channel_id=1, source_target_pairs={{0,4},{1,5},{2,6},{3,7},{4,0},{5,1},{6,2},{7,3},{8,12},{9,13},{10,... | collective-permute-start | bytes 3145736 | tf_op jit(solution)/shard_map/ppermute | solution.py:80
Sparse Core Ops, SparseCore 0:
  16.3 27.8 reduce-scatter.4
  65.1 23.8 reduce-scatter.6
  192.7 23.4 reduce-scatter.8
  235.6 25.3 reduce-scatter.10
